TPU v7x, 1024 devices: a whole 8x8x8 slice. The times are simulated.
1024 devices in a mesh: row: 64 (over x, z), col: 16 (over y, core).
Axes of the slice: x: 8, y: 8, z: 8, core: 2. Of those that a mesh axis runs over, the one named last changes fastest.
Arguments:
- kernel: bfloat16 [2048, 256, 256], P(('row', 'col')), may hold values from -0.046875 to 0.046875
- intersection: bfloat16 [32, 256, 128], replicated, may hold values from -0.375 to 0.375
- momentum: int32 [256], replicated, may hold values from 0 to 31
- owner_pick: int32 [16384], P(('row', 'col')), may hold values from 0 to 1
- live_count: int32 [1024], P(('row', 'col')), may hold values from 1 to 16, as said below
- pair_slot: int32 [16384, 4], P(('row', 'col')), may hold values from 0 to 15
- denominators: float32 [32768], P(('row', 'col')), may hold values from 0.5 to 6
- shifts: float32 [256], replicated, may hold values from 1 to 3
- vectors: bfloat16 [32768, 256], P(('row', 'col')), may hold values from -6 to 6
Outputs:
- new_vectors: float32 [32768, 256], P(('row', 'col'))
- residual: float32 [32768, 256], P(('row', 'col'))
Inputs may be any that keep to these rules, and one draw needn't show every extreme that they name: `live_count`: at most 16 incoming kernel blocks are live for a tile, and some tile has all 16 in every draw.
All inputs are finite; a program needn't handle non-finite values.
Results may differ from a plain program's by a relative error of at most 0.0037.
Values may be sent and summed in bfloat16 or wider, within the bound.
A program may use at most 32 MiB of HBM per device.

v0:
```python
import jax
import jax.numpy as jnp
from jax import lax
from jax.sharding import PartitionSpec as P


def local(
    kernel, intersection, momentum, owner_pick, live_count, pair_slot, denominators, shifts, vectors
):
    row_total = lax.axis_size("row")
    col_total = lax.axis_size("col")
    piece_rows = vectors.shape[0]
    block_size = intersection.shape[2]
    tile_rows = row_total * piece_rows
    tile_cols = col_total * piece_rows
    fine_rows = tile_rows // block_size
    fine_cols = tile_cols // block_size
    row_pos = lax.axis_index("row")
    col_pos = lax.axis_index("col")
    held_blocks, held_picks = (
        lax.all_gather(kernel, "col", axis=0, tiled=True),
        lax.all_gather(owner_pick, "col", axis=0, tiled=True),
    )
    sources = jnp.arange(col_total, dtype=jnp.int32)
    chosen = sources * kernel.shape[0] + held_picks.reshape(col_total, col_total)[:, col_pos]
    arrived = held_blocks[chosen]
    row_class = lax.dynamic_slice_in_dim(momentum, col_pos * fine_rows, fine_rows, 0)
    col_class = lax.dynamic_slice_in_dim(momentum, row_pos * fine_cols, fine_cols, 0)
    row_basis = intersection[row_class]
    col_basis = intersection[col_class]
    alive_pair = pair_slot < live_count[0]

    def one_column(column_parts):
        basis_col, slot_col, alive_col = column_parts
        half_product = lax.dot_general(
            arrived, basis_col, (((2,), (0,)), ((), ())), preferred_element_type=jnp.float32
        ).astype(jnp.bfloat16)
        picked = half_product[slot_col]
        fine_block = jnp.einsum(
            "kxa,kxf->kaf", row_basis, picked, preferred_element_type=jnp.float32
        )
        return jnp.where(alive_col[:, None, None], fine_block, jnp.zeros_like(fine_block)).astype(
            jnp.bfloat16
        )

    fine_blocks = lax.map(one_column, (col_basis, pair_slot.T, alive_pair.T))
    tile_matrix = fine_blocks.transpose(1, 2, 0, 3).reshape(tile_rows, tile_cols)

    def multiply(vector_piece):
        gathered = lax.all_gather(vector_piece, "col", axis=0, tiled=True)
        tile_part = lax.slice_in_dim(tile_matrix, 0, piece_rows * lax.axis_size("row"), axis=0)
        return lax.psum_scatter(
            jnp.dot(tile_part, gathered, preferred_element_type=jnp.float32),
            "row",
            scatter_dimension=0,
            tiled=True,
        )

    divisor = jnp.maximum(jnp.abs(denominators[:, None] - shifts[None, :]), 1.0)
    start_vectors = vectors.astype(jnp.float32)
    first_resid = multiply(vectors) - shifts[None, :] * start_vectors
    next_vectors = (start_vectors - first_resid / divisor).astype(jnp.bfloat16)
    next_float = next_vectors.astype(jnp.float32)
    second_resid = multiply(next_vectors) - shifts[None, :] * next_float
    return (next_float - second_resid / divisor, second_resid)


def solution(mesh):
    return jax.shard_map(
        local,
        mesh=mesh,
        in_specs=(
            P(("row", "col"), None, None),
            P(),
            P(),
            P(("row", "col")),
            P(("row", "col")),
            P(("row", "col"), None),
            P(("row", "col")),
            P(),
            P(("row", "col"), None),
        ),
        out_specs=(P(("row", "col"), None), P(("row", "col"), None)),
        check_vma=False,
    )
```

profile of v0, /device:TPU:1, one launch (start us, length us, event | category | flops | bytes accessed | tf_op | source)
XLA Modules:
  0.0 646.6 jit_solution(4028330497873136134)
XLA Ops:
  8.0 1.3 dynamic-slice
  10.0 0.9 dynamic-update-slice
  11.7 1.7 gather_fusion.3
  14.7 16.5 %all-reduce.1 = s32[16,16]{1,0:T(8,128)S(1)} all-reduce(s32[16,16]{1,0:T(8,128)S(1)} %reshape.49), channel_id=1, replica_groups=mesh['row'=64,'col'=16] {'col'}, use_global_device_ids=true, to_apply=%add | all-reduce | flops 256 | bytes 2048
  31.4 28.2 %all_gather.14 = bf16[512,256]{1,0:T(8,128)(2,1)} all-gather(bf16[32,256]{1,0:T(8,128)(2,1)S(1)} %copy-done.3), channel_id=1, replica_groups=mesh['row'=64,'col'=16] {'col'}, dimensions={0}, use_global_device_ids=true | all-gather | bytes 278528 | tf_op jit(solution)/shard_map/all_gather | solution.py:50
  59.6 11.2 %all-gather.2.cloned.1.call-done = bf16[32,256,256]{2,1,0:T(8,128)(2,1)} async-done(((bf16[2,256,256]{2,1,0:T(8,128)(2,1)}), bf16[32,256,256]{2,1,0:T(8,128)(2,1)}) %all-gather.2.cloned.1.call-update) | async-done | bytes 4194320 | tf_op jit(solution)/shard_map/all_gather | solution.py:21
  70.7 4.2 gather_fusion.2
  74.9 33.1 %while.10 = (s32[]{:T(128)}, bf16[4,16,128,128]{2,3,1,0:T(8,128)(2,1)}, pred[4,16]{1,0:T(4,128)(4,1)S(1)}, bf16[4,256,128]{2,1,0:T(8,128)(2,1)S(1)}, bf16[16,256...) while((s32[]{:T(128)}, bf16[4,16,128,128]{2,3,1,0:T(8,128)(2,1)}, ...), condition=%wide.region_1.2_spmd, body=%wide.region_0.1_spmd.sunk | while | flops 403702848 | bytes 10032017 | solution.py:46
  74.9 2.4 fusion.37
  77.3 1.3 copy.36
  78.7 2.0 gather_fusion
  80.7 2.5 fusion.39
  83.2 2.4 fusion.37
  85.6 1.3 copy.36
  86.9 2.0 gather_fusion
  88.9 2.5 fusion.39
  91.5 2.4 fusion.37
  93.9 1.3 copy.36
  95.2 2.0 gather_fusion
  97.2 2.5 fusion.39
  99.7 2.4 fusion.37
  102.1 1.3 copy.36
  103.4 2.0 gather_fusion
  105.4 2.6 fusion.39
  108.0 3.0 copy.23
  111.0 1.3 copy-done.1
  112.3 2.5 fusion.11
  114.9 250.4 %reduce-scatter.3.cloned.1.call-done = f32[32,256]{1,0:T(8,128)} async-done(((f32[2048,256]{1,0:T(8,128)}), f32[32,256]{1,0:T(8,128)}) %reduce-scatter.3.cloned.1.call-update) | async-done | bytes 32784 | tf_op jit(solution)/shard_map/reduce_scatter | solution.py:52
  366.1 23.1 %all_gather.15 = bf16[512,256]{1,0:T(8,128)(2,1)S(1)} all-gather(bf16[32,256]{1,0:T(8,128)(2,1)S(1)} %fusion.18), channel_id=1, replica_groups=mesh['row'=64,'col'=16] {'col'}, dimensions={0}, use_global_device_ids=true | all-gather | bytes 278528 | tf_op jit(solution)/shard_map/all_gather | solution.py:50
  389.3 4.1 fusion.9
  393.4 245.3 %reduce-scatter.5.cloned.1.call-done = f32[32,256]{1,0:T(8,128)} async-done(((f32[2048,256]{1,0:T(8,128)}), f32[32,256]{1,0:T(8,128)}) %reduce-scatter.5.cloned.1.call-update) | async-done | bytes 32784 | tf_op jit(solution)/shard_map/reduce_scatter | solution.py:52
  638.6 1.5 convert_subtract_fusion
  (45 shorter events, 3.5 us)
Async XLA Ops:
  7.2 4.5 copy-start
  7.2 6.2 copy-start.7
  7.2 24.2 %copy-start.3 = (bf16[32,256]{1,0:T(8,128)(2,1)S(1)}, bf16[32,256]{1,0:T(8,128)(2,1)}, u32[]{:S(2)}) copy-start(bf16[32,256]{1,0:T(8,128)(2,1)} %param.19) | copy-start | bytes 49156
  7.2 52.4 %copy-start.6 = (s32[16,4]{0,1:T(4,128)S(1)}, s32[16,4]{0,1:T(4,128)}, u32[]{:S(2)}) copy-start(s32[16,4]{0,1:T(4,128)} %param.16) | copy-start | bytes 772
  7.2 63.5 %all-gather.2.cloned.1.call-start = ((), (), s32[]{:S(2)}) async-start(), calls=%async_computation.2 | async-start | bytes 4456448 | tf_op jit(solution)/shard_map/all_gather | solution.py:21
  7.9 357.3 %reduce-scatter.3.cloned.1.call-start = ((), (), s32[]{:S(2)}) async-start(), calls=%async_computation.3 | async-start | bytes 2129920 | tf_op jit(solution)/shard_map/reduce_scatter | solution.py:52
  108.0 4.3 copy-start.2
  111.0 1.4 copy-start.1
  114.8 250.5 %copy-start.4 = (f32[256]{0:T(256)S(1)}, f32[256]{0:T(256)}, u32[]{:S(2)}) copy-start(f32[256]{0:T(256)} %param.18) | copy-start | bytes 3076
  114.8 250.5 %copy-start.5 = (f32[32]{0:T(128)S(1)}, f32[32]{0:T(128)}, u32[]{:S(2)}) copy-start(f32[32]{0:T(128)} %param.17) | copy-start | bytes 388
  114.9 523.8 %reduce-scatter.5.cloned.1.call-start = ((), (), s32[]{:S(2)}) async-start(), calls=%async_computation.4 | async-start | bytes 2129920 | tf_op jit(solution)/shard_map/reduce_scatter | solution.py:52
Sparse Core Ops, SparseCore 0:
  10.7 59.9 all-gather.1
  115.0 250.2 reduce-scatter.2
  393.5 245.0 reduce-scatter.4
where the time goes:
time: 651 us; the launch traced here: 647 us
  waiting for transfers between devices  508 us (78%)
  blocking collectives  67.8 us (10%)
  local copies, waits for them, and re-layouts  26.3 us (4%)
  matrix products  26.3 us (4%)
  between operations  15.2 us (2%)
    reduce_scatter x2, waiting for transfers between devices, multiply(): lax.psum_scatter(jnp.dot(tile_part, gathered, preferred_element_type=jnp....  496 us
    all_gather x2, blocking collectives, multiply(): gathered = lax.all_gather(vector_piece, 'col', axis=0, tiled=True)  51.3 us
    unnamed x1, blocking collectives  16.5 us
  transfers between devices with their start and end apart: 3, of which 3 were waited for; matrix products, arithmetic and copies ran while one was open for 1% of the time, Pallas kernels for 0%

commit v1 on v0

v1 whole, which is shorter than its diff:
```python
import functools

import jax
import jax.numpy as jnp
from jax import lax
from jax.experimental import pallas as pl
from jax.experimental.pallas import tpu as pltpu
from jax.sharding import PartitionSpec as P

F32 = jnp.float32
BF16 = jnp.bfloat16


def send(src, dst, send_sem, recv_sem, row, col):
    return pltpu.make_async_remote_copy(
        src_ref=src,
        dst_ref=dst,
        send_sem=send_sem,
        recv_sem=recv_sem,
        device_id={"row": row, "col": col},
        device_id_type=pl.DeviceIdType.MESH,
    )


def body(
    nx, nz, ny, fb,
    mom, picks, live, slots, inter_hbm, kern_hbm, den, shifts, vec,
    prod_out, next_out,
    inter, blk, half, basis, tile, held, nextv, pk, pk_own,
    part0, part1, rx0, rx1, ry0, ry1, sum0, sum1, acc0, acc1,
    loc, pk_s, pk_r, ag_s, ag_r, fw_s, fw_r, ring_s, ring_r, sib_s, sib_r, s1_s, s1_r, s2_s, s2_r,
):
    nc = 2 * ny
    pr = vec.shape[0]
    nv = vec.shape[1]
    hv = nv // 2
    fc = nc * pr // fb
    chunk = nz * pr
    nblk = chunk // fb
    hop = ny // 2

    row = lax.axis_index("row")
    c = lax.axis_index("col")
    x, z = row // nz, row % nz
    y, core = c // 2, c % 2
    other = y * 2 + (1 - core)

    copy_kern = pltpu.make_async_copy(kern_hbm, blk.at[c], loc.at[0])
    copy_inter = pltpu.make_async_copy(inter_hbm, inter, loc.at[1])
    copy_kern.start()
    copy_inter.start()

    lane = lax.broadcasted_iota(jnp.int32, (8, 128), 1)
    mine = jnp.zeros((8, 128), jnp.int32)
    for j in range(nc):
        mine = jnp.where(lane == j, picks[j], mine)
    pk_own[...] = mine
    pk[c] = mine

    barrier = pltpu.get_barrier_semaphore()
    for d in range(1, nc):
        pl.semaphore_signal(barrier, inc=1, device_id={"row": row, "col": (c + d) % nc}, device_id_type=pl.DeviceIdType.MESH)
    for d in range(1, nx):
        pl.semaphore_signal(barrier, inc=1, device_id={"row": ((x + d) % nx) * nz + z, "col": c}, device_id_type=pl.DeviceIdType.MESH)
    for d in range(1, nz):
        pl.semaphore_signal(barrier, inc=1, device_id={"row": x * nz + (z + d) % nz, "col": c}, device_id_type=pl.DeviceIdType.MESH)
    pl.semaphore_wait(barrier, nc - 1 + nx - 1 + nz - 1)

    pending = []

    pk_copies = []
    for d in range(1, nc):
        cp = send(pk_own, pk.at[c], pk_s.at[d], pk_r.at[d], row, (c + d) % nc)
        cp.start()
        pk_copies.append(cp)
    pending += pk_copies

    def order(n):
        return [n // 2 + ((i + 1) // 2) * (1 - 2 * (i % 2)) for i in range(n - 1)]

    def gather_start(p, src):
        copies = {}
        for d in order(ny):
            copies[d] = send(src, held.at[p, pl.ds(c * pr, pr)], ag_s.at[p, d], ag_r.at[p, d], row, ((y + d) % ny) * 2 + core)
            copies[d].start()
        copies[0] = send(src, held.at[p, pl.ds(c * pr, pr)], ag_s.at[p, 0], ag_r.at[p, 0], row, other)
        copies[0].start()
        held[p, pl.ds(c * pr, pr), :] = src[...]
        return copies

    def gather_relay(p, copies):
        for d in sorted(range(1, ny), key=lambda d: min(d, ny - d)):
            copies[d].wait_recv()
            rows = pl.ds((((y - d) % ny) * 2 + core) * pr, pr)
            cp = send(held.at[p, rows], held.at[p, rows], fw_s.at[p, d], fw_r.at[p, d], row, other)
            cp.start()
            copies[ny + d] = cp

    def gather_end(p, copies):
        copies[0].wait_recv()
        for d in range(1, ny):
            copies[ny + d].wait_recv()

    got0 = gather_start(0, vec)

    length = {(0, 0): hop, (0, 1): hop - 1, (1, 0): hop - 1, (1, 1): hop}
    lanes = [(0, 0), (1, 1), (0, 1), (1, 0)]
    step_to = [((y + 1) % ny) * 2 + core, ((y + ny - 1) % ny) * 2 + core]

    def source(way, t):
        return ((y - t) % ny if way == 0 else (y + t) % ny) * 2 + core

    ring = {}
    for way, k in lanes:
        if length[way, k] >= 1:
            cp = send(kern_hbm.at[k], blk.at[c, k], ring_s.at[way, 0, k], ring_r.at[way, 0, k], row, step_to[way])
            cp.start()
            ring[way, 1, k] = cp
    sib = {}
    for k in range(2):
        cp = send(kern_hbm.at[k], blk.at[c, k], sib_s.at[0, 0, k], sib_r.at[0, 0, k], row, other)
        cp.start()
        sib[0, 0, k] = cp

    copy_kern.wait()
    copy_inter.wait()
    for b in range(fc):
        basis[:, b * fb:(b + 1) * fb] = inter[mom[row * fc + b]]
    half[nc] = jnp.zeros(half.shape[1:], BF16)
    for cp in pk_copies:
        cp.wait_recv()

    wide = fc * fb
    cut = min(wide, 2 * fb)

    def half_of(src):
        flag = jnp.sum(jnp.where(lax.broadcasted_iota(jnp.int32, (1, 128), 1) == c, pk[src][0:1, :], 0).astype(F32), axis=1, keepdims=True)
        for j in range(wide // cut):
            cols = slice(j * cut, (j + 1) * cut)
            second = jnp.broadcast_to(flag, (blk.shape[2], cut)) > 0.5
            h0 = jnp.dot(blk[src, 0], basis[:, cols], preferred_element_type=F32)
            h1 = jnp.dot(blk[src, 1], basis[:, cols], preferred_element_type=F32)
            half[src, :, cols] = jnp.where(second, h1, h0).astype(BF16)

    def halves(t):
        ways = [0] if t == 0 else [0, 1]
        for way in ways:
            for k in range(2):
                if (way, t, k) in sib:
                    sib[way, t, k].wait_recv()
        if t == 0 or t == hop:
            spot = y if t == 0 else (y + hop) % ny

            def one(j, carry):
                half_of(spot * 2 + j)
                return carry

            lax.fori_loop(0, 2, one, 0)
        else:

            def one(j, carry):
                half_of(((y + ny + (1 - 2 * (j // 2)) * t) % ny) * 2 + j % 2)
                return carry

            lax.fori_loop(0, 4, one, 0)

    for t in range(1, hop + 1):
        for way, k in lanes:
            if t > length[way, k]:
                continue
            ring[way, t, k].wait_recv()
            src = source(way, t)
            if t < length[way, k]:
                cp = send(blk.at[src, k], blk.at[src, k], ring_s.at[way, t, k], ring_r.at[way, t, k], row, step_to[way])
                cp.start()
                ring[way, t + 1, k] = cp
            cp = send(blk.at[src, k], blk.at[src, k], sib_s.at[way, t, k], sib_r.at[way, t, k], row, other)
            cp.start()
            sib[way, t, k] = cp
        if t == 1:
            gather_relay(0, got0)
        halves(t - 1)
    halves(hop)
    pending += list(ring.values()) + list(sib.values()) + list(got0.values())
    gather_end(0, got0)

    def offset(i, n):
        return n // 2 + ((i + 1) // 2) * (1 - 2 * (i % 2))

    def reduce_rows(p):
        v = held[p]

        def rows_for(x2):
            for q in range(nblk):
                a = x2 * nblk + q
                rows = pl.ds(pl.multiple_of(a * fb, fb), fb)
                if p == 0:
                    parts = []
                    for b in range(fc):
                        slot = slots[a, b]
                        slot = jnp.where(slot < live[0], slot, nc)
                        parts.append(half[slot, :, b * fb:(b + 1) * fb])
                    picked = jnp.concatenate(parts, axis=1)
                    u = inter[mom[c * (nx * nblk) + a]]
                    fine = lax.dot_general(u, picked, (((0,), (0,)), ((), ())), preferred_element_type=F32)
                    tile[rows, :] = fine.astype(BF16)
                got = jnp.dot(tile[rows, :], v, preferred_element_type=F32).astype(BF16)
                part0[p, rows, :] = got[:, :hv]
                for j in range(fb // pr):
                    z2 = q * (fb // pr) + j
                    part1[p, z2, pl.ds(pl.multiple_of(x2 * pr, pr), pr), :] = got[j * pr:(j + 1) * pr, hv:]

        def x_copy(i):
            d = offset(i, nx)
            x2 = (x + d) % nx
            return send(part0.at[p, pl.ds(pl.multiple_of(x2 * chunk, chunk), chunk)], rx0.at[p, d], s1_s.at[p, 0, d], s1_r.at[p, 0, d], x2 * nz + z, c)

        def step(i, carry):
            rows_for((x + offset(i, nx)) % nx)
            x_copy(i).start()
            return carry

        if nx > 1:
            lax.fori_loop(0, nx - 1, step, 0)
        rows_for(x)

        def z_copy(d):
            z2 = (z + d) % nz
            return send(part1.at[p, z2], rx1.at[p, d], s1_s.at[p, 1, d], s1_r.at[p, 1, d], x * nz + z2, c)

        z_copies = {d: z_copy(d) for d in order(nz)}
        for d in order(nz):
            z_copies[d].start()
        x_copies = {offset(i, nx): x_copy(i) for i in range(nx - 1)}

        acc0[...] = part0[p, pl.ds(pl.multiple_of(x * chunk, chunk), chunk), :].astype(F32)
        acc1[...] = part1[p, z].astype(F32)
        for d in order(nx):
            x_copies[d].wait_recv()
            acc0[...] += rx0[p, d].astype(F32)
        sum0[p] = acc0[...].astype(BF16)
        last0 = {}
        for d in order(nz):
            z2 = (z + d) % nz
            last0[d] = send(sum0.at[p, pl.ds(pl.multiple_of(z2 * pr, pr), pr)], ry0.at[p, d], s2_s.at[p, 0, d], s2_r.at[p, 0, d], x * nz + z2, c)
            last0[d].start()
        for d in order(nz):
            z_copies[d].wait_recv()
            acc1[...] += rx1[p, d].astype(F32)
        sum1[p] = acc1[...].astype(BF16)
        last1 = {}
        for d in order(nx):
            x2 = (x + d) % nx
            last1[d] = send(sum1.at[p, pl.ds(pl.multiple_of(x2 * pr, pr), pr)], ry1.at[p, d], s2_s.at[p, 1, d], s2_r.at[p, 1, d], x2 * nz + z, c)
            last1[d].start()
        total0 = acc0[pl.ds(pl.multiple_of(z * pr, pr), pr), :]
        for d in order(nz):
            last0[d].wait_recv()
            total0 += ry0[p, d].astype(F32)
        total1 = acc1[pl.ds(pl.multiple_of(x * pr, pr), pr), :]
        for d in order(nx):
            last1[d].wait_recv()
            total1 += ry1[p, d].astype(F32)
        pending.extend(list(x_copies.values()) + list(z_copies.values()) + list(last0.values()) + list(last1.values()))
        return total0, total1

    eye = lax.broadcasted_iota(jnp.int32, (pr, pr), 0) == lax.broadcasted_iota(jnp.int32, (pr, pr), 1)
    den_col = jnp.sum(jnp.where(eye, jnp.broadcast_to(den[...], (pr, pr)), 0.0), axis=1, keepdims=True)

    totals = reduce_rows(0)
    for h in range(2):
        cols = slice(h * hv, (h + 1) * hv)
        sh = shifts[:, cols]
        start = vec[:, cols].astype(F32)
        resid = totals[h] - sh * start
        div = jnp.maximum(jnp.abs(den_col - sh), 1.0)
        nextv[:, cols] = (start - resid / div).astype(BF16)
    got1 = gather_start(1, nextv)
    gather_relay(1, got1)
    gather_end(1, got1)
    pending += list(got1.values())
    totals = reduce_rows(1)
    for h in range(2):
        prod_out[:, h * hv:(h + 1) * hv] = totals[h]
    next_out[...] = nextv[...]
    for cp in pending:
        cp.wait_send()


def local(nx, nz, ny, kernel, intersection, momentum, owner_pick, live_count, pair_slot, denominators, shifts, vectors):
    pr, nv = vectors.shape
    nq, cb, fb = intersection.shape
    nc = 2 * ny
    hv = nv // 2
    rows = nx * nz * pr
    wide = nc * pr
    hop = ny // 2
    dma = pltpu.SemaphoreType.DMA
    smem = pl.BlockSpec(memory_space=pltpu.SMEM)
    anyspace = pl.BlockSpec(memory_space=pl.ANY)
    vmem = pl.BlockSpec(memory_space=pltpu.VMEM)
    far = max(nx, nz)
    prod, nextv = pl.pallas_call(
        functools.partial(body, nx, nz, ny, fb),
        out_shape=(jax.ShapeDtypeStruct((pr, nv), F32), jax.ShapeDtypeStruct((pr, nv), BF16)),
        in_specs=[smem, smem, smem, smem, anyspace, anyspace, vmem, vmem, vmem],
        out_specs=(vmem, vmem),
        scratch_shapes=[
            pltpu.VMEM((nq, cb, fb), BF16),
            pltpu.VMEM((nc, 2, cb, cb), BF16),
            pltpu.VMEM((nc + 1, cb, wide), BF16),
            pltpu.VMEM((cb, wide), BF16),
            pltpu.VMEM((rows, wide), BF16),
            pltpu.VMEM((2, wide, nv), BF16),
            pltpu.VMEM((pr, nv), BF16),
            pltpu.VMEM((nc, 8, 128), jnp.int32),
            pltpu.VMEM((8, 128), jnp.int32),
            pltpu.VMEM((2, rows, hv), BF16),
            pltpu.VMEM((2, nz, nx * pr, hv), BF16),
            pltpu.VMEM((2, nx, nz * pr, hv), BF16),
            pltpu.VMEM((2, nz, nx * pr, hv), BF16),
            pltpu.VMEM((2, nz, pr, hv), BF16),
            pltpu.VMEM((2, nx, pr, hv), BF16),
            pltpu.VMEM((2, nz * pr, hv), BF16),
            pltpu.VMEM((2, nx * pr, hv), BF16),
            pltpu.VMEM((nz * pr, hv), F32),
            pltpu.VMEM((nx * pr, hv), F32),
            dma((2,)),
            dma((nc,)), dma((nc,)),
            dma((2, ny)), dma((2, ny)),
            dma((2, ny)), dma((2, ny)),
            dma((2, hop, 2)), dma((2, hop, 2)),
            dma((2, hop + 1, 2)), dma((2, hop + 1, 2)),
            dma((2, 2, far)), dma((2, 2, far)),
            dma((2, 2, far)), dma((2, 2, far)),
        ],
        compiler_params=pltpu.CompilerParams(collective_id=0, has_side_effects=True, vmem_limit_bytes=48 * 1024 * 1024),
    )(
        momentum, owner_pick, live_count, pair_slot, intersection, kernel,
        denominators.reshape(1, pr), shifts.reshape(1, nv), vectors,
    )
    next_float = nextv.astype(F32)
    divisor = jnp.maximum(jnp.abs(denominators[:, None] - shifts[None, :]), 1.0)
    residual = prod - shifts[None, :] * next_float
    return next_float - residual / divisor, residual


def build(mesh, nx, nz, ny):
    whole = P(("row", "col"))
    return jax.shard_map(
        functools.partial(local, nx, nz, ny),
        mesh=mesh,
        in_specs=(
            P(("row", "col"), None, None), P(), P(), whole, whole, P(("row", "col"), None), whole, P(), P(("row", "col"), None),
        ),
        out_specs=(P(("row", "col"), None), P(("row", "col"), None)),
        check_vma=False,
    )


def solution(mesh):
    return build(mesh, 8, 8, mesh.shape["col"] // 2)
```

time: 651 us -> 110 us (0.17)
  waiting for transfers between devices: 508 us -> 0 us
  Pallas kernels: 0 us -> 101 us
  blocking collectives: 67.8 us -> 0 us
  matrix products: 26.3 us -> 0 us
  local copies, waits for them, and re-layouts: 26.3 us -> 6.68 us
  between operations: 15.2 us -> 1.29 us
    reduce_scatter x2 -> x0, waiting for transfers between devices: 496 us -> none  [multiply(): lax.psum_scatter(jnp.dot(tile_part, gathered, preferred_element_type=jnp....]
    pallas_call x0 -> x1, Pallas kernels: none -> 101 us  [local(): pl.pallas_call(functools.partial(body, nx, nz, ny, fb), out_shape=(jax.Sh...]
    all_gather x2 -> x0, blocking collectives: 51.3 us -> none  [multiply(): gathered = lax.all_gather(vector_piece, 'col', axis=0, tiled=True)]
    dot_general x10 -> x0, matrix products: 26.3 us -> none  [the longest x4 10.1 us: one_column(): jnp.einsum('kxa,kxf->kaf', row_basis, picked, preferred_element_type=jnp....]
    unnamed x1 -> x0, blocking collectives: 16.5 us -> none
    gather x7 -> x0, local copies, waits for them, and re-layouts: 14.4 us -> none  [the longest x4 7.89 us: one_column(): picked = half_product[slot_col]]
    all_gather x1 -> x0, waiting for transfers between devices: 11.2 us -> none  [local(): lax.all_gather(kernel, 'col', axis=0, tiled=True)]
  transfers between devices with their start and end apart: 3 -> 0, of which waited for: 3 -> 0; matrix products, arithmetic and copies ran while one was open for 1% -> 0% of each run, Pallas kernels for 0% -> 0%
where the time goes in v1:
time: 110 us
  Pallas kernels  101 us (92%)
  local copies, waits for them, and re-layouts  6.68 us (6%)
  between operations  1.29 us (1%)
    pallas_call x1, Pallas kernels, local(): pl.pallas_call(functools.partial(body, nx, nz, ny, fb), out_shape=(jax.Sh...  101 us
    unnamed x15, local copies, waits for them, and re-layouts  6.68 us

profile of v1, /device:TPU:1, one launch (start us, length us, event | category | flops | bytes accessed | tf_op | source)
XLA Modules:
  0.0 109.8 jit_solution(18424300709674572059)
XLA Ops:
  1.3 0.8 copy.11.slots
  2.0 0.0 copy-start
  2.0 1.6 %copy-done = bf16[32,256,128]{2,1,0:T(8,128)(2,1)S(1)} copy-done((bf16[32,256,128]{2,1,0:T(8,128)(2,1)S(1)}, bf16[32,256,128]{2,1,0:T(8,128)(2,1)}, u32[]{:S(2)}) %copy-start) | copy-done | bytes 2097176
  3.6 0.0 copy-start.1
  3.6 0.9 copy-done.1
  4.6 0.0 copy-start.2
  4.6 0.7 copy-done.2
  5.3 0.0 copy-start.3
  5.3 0.7 copy-done.3
  6.0 0.0 copy-start.4
  6.0 0.7 copy-done.4
  6.6 0.0 copy-start.5
  6.6 0.7 copy-done.5
  7.3 0.0 copy-start.6
  7.3 0.7 copy-done.6
  8.0 101.1 %shard_map.104 = (f32[32,256]{1,0:T(8,128)S(1)}, bf16[32,256]{1,0:T(8,128)(2,1)S(1)}) custom-call(s32[256]{0:T(256)S(1)} %copy-done.5, s32[16]{0:T(128)S(1)} %copy-done.6, s32[1]{0:T(128)S(6)} %copy.12.live, s32[16,4]{1,0:T(8,128)S(1)} %copy.11.slots, bf16[32,256,128]{2,1,0:T(8,128)(2,1)S(1)} %copy-done, bf16[2,256,256]{2,1,0:T(8,128)(2,1)S(1)} %copy-done.1, ...), custom_call_target="tpu_custom_call" | custom-call | tf_op jit(solution)/shard_map/pallas_call | solution.py:303
  109.1 0.7 convert_subtract_fusion
Async XLA Ops:
  2.0 1.6 %copy-start = (bf16[32,256,128]{2,1,0:T(8,128)(2,1)S(1)}, bf16[32,256,128]{2,1,0:T(8,128)(2,1)}, u32[]{:S(2)}) copy-start(bf16[32,256,128]{2,1,0:T(8,128)(2,1)} %inter_hbm.1) | copy-start | bytes 6291460
  3.6 0.9 copy-start.1
  4.6 0.7 copy-start.2
  5.3 0.7 copy-start.3
  6.0 0.7 copy-start.4
  6.6 0.7 copy-start.5
  7.3 0.7 copy-start.6

commit v2 on v1

v2 whole, which is shorter than its diff:
```python
import functools

import jax
import jax.numpy as jnp
from jax import lax
from jax.experimental import pallas as pl
from jax.experimental.pallas import tpu as pltpu
from jax.sharding import PartitionSpec as P

F32 = jnp.float32
BF16 = jnp.bfloat16


def send(src, dst, send_sem, recv_sem, row, col):
    return pltpu.make_async_remote_copy(
        src_ref=src,
        dst_ref=dst,
        send_sem=send_sem,
        recv_sem=recv_sem,
        device_id={"row": row, "col": col},
        device_id_type=pl.DeviceIdType.MESH,
    )


def body(
    nx, nz, ny, fb,
    mom_hbm, picks_hbm, live_hbm, slots_hbm, inter_hbm, kern_hbm, den_hbm, shifts_hbm, vec_hbm,
    prod_out, next_out,
    mom, picks, live, slots, den, shifts, vec,
    inter, blk, half, basis, tile, held, heldn, nextv, pk, pk_own,
    part0, part1, near0, near1, pair0, pair1, rx0, rx1, ry0, ry1, sum0, sum1, acc0, acc1,
    loc, ag_s, ag_r, fw_s, fw_r, ring_s, ring_r, sib_s, sib_r, ringp_s, ringp_r, sibp_s, sibp_r,
    s0_s, s0_r, s1_s, s1_r, s2_s, s2_r,
):
    nc = 2 * ny
    pr, nv = vec.shape
    gv = nv // 2
    hr = pr // 2
    fc = nc * pr // fb
    chunk = nz * pr
    nblk = chunk // fb
    hop = ny // 2

    row = lax.axis_index("row")
    c = lax.axis_index("col")
    x, z = row // nz, row % nz
    y, core = c // 2, c % 2
    other = y * 2 + (1 - core)

    def bring(i, src, dst):
        cp = pltpu.make_async_copy(src, dst, loc.at[i])
        cp.start()
        return cp

    get_picks = bring(0, picks_hbm, picks)
    get_vec = bring(1, vec_hbm, vec)
    cb = kern_hbm.shape[1]
    own = []
    for k in range(2):
        own.append(bring(2 + 2 * k, kern_hbm.at[k], blk.at[c, k, pl.ds(0, cb)]))
        own.append(bring(3 + 2 * k, vec_hbm.at[pl.ds(k * hr, hr), pl.ds(0, cb)], blk.at[c, k, pl.ds(cb, hr)]))
    get_mom = bring(6, mom_hbm, mom)
    get_inter = bring(7, inter_hbm, inter)
    late = [bring(8, live_hbm, live), bring(9, slots_hbm, slots), bring(10, den_hbm, den), bring(11, shifts_hbm, shifts)]

    barrier = pltpu.get_barrier_semaphore()

    def greet(to_row, to_col):
        pl.semaphore_signal(barrier, inc=1, device_id={"row": to_row, "col": to_col}, device_id_type=pl.DeviceIdType.MESH)

    for d in range(1, nx):
        greet(((x + d) % nx) * nz + z, c)
    for d in range(1, nz):
        greet(x * nz + (z + d) % nz, c)
    for d in range(1, ny):
        greet(row, ((y + d) % ny) * 2 + core)
    greet(row, other)

    get_picks.wait()
    lane = lax.broadcasted_iota(jnp.int32, (8, 128), 1)
    mine = jnp.zeros((8, 128), jnp.int32)
    for j in range(nc):
        mine = jnp.where(lane == j, picks[j], mine)
    pk_own[...] = mine
    pk[c] = mine

    for cp in own:
        cp.wait()
    pl.semaphore_wait(barrier, nx - 1 + nz - 1 + ny - 1 + 1)

    pending = []

    def order(n):
        return [n // 2 + ((i + 1) // 2) * (1 - 2 * (i % 2)) for i in range(n - 1)]

    length = {(0, 0): hop, (0, 1): hop - 1, (1, 0): hop - 1, (1, 1): hop}
    lanes = [(0, 0), (1, 1), (0, 1), (1, 0)]
    step_to = [((y + 1) % ny) * 2 + core, ((y + ny - 1) % ny) * 2 + core]

    def source(way, t):
        return ((y - t) % ny if way == 0 else (y + t) % ny) * 2 + core

    def pass_on(way, t, k, src, to, sems):
        bs, br, ps, pq = sems
        out = [send(blk.at[src, k], blk.at[src, k], bs.at[way, t, k], br.at[way, t, k], row, to)]
        if k == 0:
            from_pk = pk_own if t == 0 else pk.at[src]
            out.append(send(from_pk.at[pl.ds(0, 1)], pk.at[src, pl.ds(0, 1)], ps.at[way, t], pq.at[way, t], row, to))
        for cp in out:
            cp.start()
        return out

    on_ring = (ring_s, ring_r, ringp_s, ringp_r)
    on_sib = (sib_s, sib_r, sibp_s, sibp_r)
    ring, sib = {}, {}
    for way, k in lanes:
        if length[way, k] >= 1:
            ring[way, 1, k] = pass_on(way, 0, k, c, step_to[way], on_ring)
    for k in range(2):
        sib[0, 0, k] = pass_on(0, 0, k, c, other, on_sib)

    get_mom.wait()
    get_inter.wait()
    get_vec.wait()
    for b in range(fc):
        basis[:, b * fb:(b + 1) * fb] = inter[mom[row * fc + b]]
    half[nc] = jnp.zeros(half.shape[1:], BF16)
    for cp in late:
        cp.wait()

    wide = fc * fb
    cut = min(wide, 2 * fb)

    def half_of(src):
        flag = jnp.sum(jnp.where(lax.broadcasted_iota(jnp.int32, (1, 128), 1) == c, pk[src][0:1, :], 0).astype(F32), axis=1, keepdims=True)
        for j in range(wide // cut):
            cols = slice(j * cut, (j + 1) * cut)
            second = jnp.broadcast_to(flag, (cb, cut)) > 0.5
            h0 = jnp.dot(blk[src, 0, 0:cb], basis[:, cols], preferred_element_type=F32)
            h1 = jnp.dot(blk[src, 1, 0:cb], basis[:, cols], preferred_element_type=F32)
            half[src, :, cols] = jnp.where(second, h1, h0).astype(BF16)
        for k in range(2):
            held[pl.ds(pl.multiple_of(src * pr + k * hr, hr), hr), :] = blk[src, k, cb:cb + hr]

    def halves(t):
        for way in range(1 if t == 0 else 2):
            for k in range(2):
                for cp in sib.get((way, t, k), []):
                    cp.wait_recv()
        if t == 0 or t == hop:
            spot = y if t == 0 else (y + hop) % ny

            def one(j, carry):
                half_of(spot * 2 + j)
                return carry

            lax.fori_loop(0, 2, one, 0)
        else:

            def one(j, carry):
                half_of(((y + ny + (1 - 2 * (j // 2)) * t) % ny) * 2 + j % 2)
                return carry

            lax.fori_loop(0, 4, one, 0)

    for t in range(1, hop + 1):
        for way, k in lanes:
            if t > length[way, k]:
                continue
            src = source(way, t)
            for cp in ring[way, t, k]:
                cp.wait_recv()
            if t < length[way, k]:
                ring[way, t + 1, k] = pass_on(way, t, k, src, step_to[way], on_ring)
            sib[way, t, k] = pass_on(way, t, k, src, other, on_sib)
        halves(t - 1)
    halves(hop)
    for many in list(ring.values()) + list(sib.values()):
        pending += many

    sense = 1 - 2 * core

    def pairs_of(n):
        pairs = [(s, s - 1) for s in range(n // 2, 1, -2)]
        pairs += [(-s, 1 - s) for s in range(n // 2 - 1, 1, -2)]
        taken = {s for pair in pairs for s in pair}
        return pairs, [s for s in [*range(1 - n // 2, 0), *range(1, n // 2 + 1)] if s not in taken]

    def dest(i, s, n):
        return (i + n - sense * s) % n

    def table(values, i, n):
        packed = sum((v % n) << (3 * j) for j, v in enumerate(values))
        return (jnp.int32(packed) >> (3 * i)) & 7

    def tile_rows(x2):
        return pl.ds(pl.multiple_of(x2 * chunk, chunk), chunk)

    def build_rows(x2):
        for q in range(nblk):
            a = x2 * nblk + q
            parts = []
            for b in range(fc):
                slot = slots[b, a]
                slot = jnp.where(slot < live[0], slot, nc)
                parts.append(half[slot, :, b * fb:(b + 1) * fb])
            picked = jnp.concatenate(parts, axis=1)
            u = inter[mom[c * (nx * nblk) + a]]
            fine = lax.dot_general(u, picked, (((0,), (0,)), ((), ())), preferred_element_type=F32)
            tile[pl.ds(pl.multiple_of(a * fb, fb), fb), :] = fine.astype(BF16)

    flight = {}

    def spread(p, g, build):
        def product(x2):
            if build:
                build_rows(x2)
            v = held[:, g * gv:(g + 1) * gv] if p == 0 else heldn[g]
            got = jnp.dot(tile[tile_rows(x2), :], v, preferred_element_type=F32).astype(BF16)
            for j in range(nz):
                part0[p, g, x2, j * hr:(j + 1) * hr, :] = got[j * pr:j * pr + hr]
                part1[p, g, j, pl.ds(pl.multiple_of(x2 * hr, hr), hr), :] = got[j * pr + hr:(j + 1) * pr]

        def far_copy(h, j, far, near):
            n, me = (nx, x) if h == 0 else (nz, z)
            to = (me + n + sense * (near - far)) % n
            part, into = (part0, near0) if h == 0 else (part1, near1)
            return send(part.at[p, g, dest(me, far, n)], into.at[p, g, j], s0_s.at[p, g, h, j], s0_r.at[p, g, h, j],
                        to * nz + z if h == 0 else x * nz + to, c)

        def step(i, carry):
            product(dest(x, table(order_of, i + start, nx), nx))
            return carry

        pairs, singles = pairs_of(nx)
        order_of = [far for far, near in pairs] + singles + [near for far, near in pairs] + [0]

        fars = {}
        start = 0
        for j, (far, near) in enumerate(pairs):
            fars[0, j] = far_copy(0, j, far, near)
        if pairs:

            def far_step(i, carry):
                far = table(order_of, i, nx)
                product(dest(x, far, nx))
                turn = table([(near - far) for far, near in pairs], i, nx)
                to = (x + nx + sense * turn) % nx
                send(part0.at[p, g, dest(x, far, nx)], near0.at[p, g, i], s0_s.at[p, g, 0, i], s0_r.at[p, g, 0, i], to * nz + z, c).start()
                return carry

            lax.fori_loop(0, len(pairs), far_step, 0)
        start = len(pairs)
        lax.fori_loop(0, nx - len(pairs), step, 0)
        direct = {}
        for h in range(2):
            n, me = (nx, x) if h == 0 else (nz, z)
            pairs, singles = pairs_of(n)
            if h == 1:
                for j, (far, near) in enumerate(pairs):
                    fars[1, j] = far_copy(1, j, far, near)
                    fars[1, j].start()
            part, rx = (part0, rx0) if h == 0 else (part1, rx1)
            for j, s in enumerate(singles):
                to = dest(me, s, n)
                cp = send(part.at[p, g, to], rx.at[p, g, len(pairs) + j], s1_s.at[p, g, h, len(pairs) + j], s1_r.at[p, g, h, len(pairs) + j],
                          to * nz + z if h == 0 else x * nz + to, c)
                cp.start()
                direct[h, len(pairs) + j] = cp
        flight[p, g] = [fars, direct]

    def relay(p, g):
        fars, direct = flight[p, g]
        for j in range(max(len(pairs_of(nx)[0]), len(pairs_of(nz)[0]))):
            for h in range(2):
                n, me = (nx, x) if h == 0 else (nz, z)
                pairs = pairs_of(n)[0]
                if j >= len(pairs):
                    continue
                to = dest(me, pairs[j][1], n)
                part, near, pair, rx = (part0, near0, pair0, rx0) if h == 0 else (part1, near1, pair1, rx1)
                fars[h, j].wait_recv()
                pair[p, g, j] = (part[p, g, to].astype(F32) + near[p, g, j].astype(F32)).astype(BF16)
                direct[h, j] = send(pair.at[p, g, j], rx.at[p, g, j], s1_s.at[p, g, h, j], s1_r.at[p, g, h, j],
                                    to * nz + z if h == 0 else x * nz + to, c)
                direct[h, j].start()

    def first_sums(p, g):
        direct = flight[p, g][1]
        last0, last1 = {}, {}
        for h in range(2):
            part, acc, rx, total = (part0, acc0, rx0, sum0) if h == 0 else (part1, acc1, rx1, sum1)
            sums = part[p, g, x if h == 0 else z].astype(F32)
            for j in sorted((j for way, j in direct if way == h), reverse=True):
                direct[h, j].wait_recv()
                sums += rx[p, g, j].astype(F32)
            acc[g] = sums
            total[p, g] = sums.astype(BF16)
            for d in order(nz if h == 0 else nx):
                to = (z + d) % nz if h == 0 else (x + d) % nx
                rows = pl.ds(pl.multiple_of(to * hr, hr), hr)
                if h == 0:
                    last0[d] = send(sum0.at[p, g, rows], ry0.at[p, g, d], s2_s.at[p, g, 0, d], s2_r.at[p, g, 0, d], x * nz + to, c)
                    last0[d].start()
                else:
                    last1[d] = send(sum1.at[p, g, rows], ry1.at[p, g, d], s2_s.at[p, g, 1, d], s2_r.at[p, g, 1, d], to * nz + z, c)
                    last1[d].start()
        flight[p, g] += [last0, last1]

    def last_sums(p, g):
        last0, last1 = flight[p, g][2:]
        total0 = acc0[g, pl.ds(pl.multiple_of(z * hr, hr), hr), :]
        for d, cp in last0.items():
            cp.wait_recv()
            total0 += ry0[p, g, d].astype(F32)
        total1 = acc1[g, pl.ds(pl.multiple_of(x * hr, hr), hr), :]
        for d, cp in last1.items():
            cp.wait_recv()
            total1 += ry1[p, g, d].astype(F32)
        for copies in flight[p, g]:
            pending.extend(copies.values())
        return jnp.concatenate([total0, total1], axis=0)

    mine_rows = pl.ds(pl.multiple_of(c * pr, pr), pr)

    def gather_start(g):
        copies = {}
        for d in order(ny):
            copies[d] = send(nextv.at[g], heldn.at[g, mine_rows], ag_s.at[g, d], ag_r.at[g, d], row, ((y + d) % ny) * 2 + core)
            copies[d].start()
        copies[0] = send(nextv.at[g], heldn.at[g, mine_rows], ag_s.at[g, 0], ag_r.at[g, 0], row, other)
        copies[0].start()
        return copies

    def gather_relay(g, copies):
        for d in sorted(range(1, ny), key=lambda d: min(d, ny - d)):
            copies[d].wait_recv()
            rows = pl.ds(pl.multiple_of((((y - d) % ny) * 2 + core) * pr, pr), pr)
            cp = send(heldn.at[g, rows], heldn.at[g, rows], fw_s.at[g, d], fw_r.at[g, d], row, other)
            cp.start()
            copies[ny + d] = cp

    def gather_end(g, copies):
        copies[0].wait_recv()
        for d in range(1, ny):
            copies[ny + d].wait_recv()
        pending.extend(copies.values())

    eye = lax.broadcasted_iota(jnp.int32, (pr, pr), 0) == lax.broadcasted_iota(jnp.int32, (pr, pr), 1)
    den_col = jnp.sum(jnp.where(eye, jnp.broadcast_to(den[...], (pr, pr)), 0.0), axis=1, keepdims=True)

    spread(0, 0, True)
    spread(0, 1, False)
    for g in range(2):
        relay(0, g)
    for g in range(2):
        first_sums(0, g)
    got = []
    for g in range(2):
        total = last_sums(0, g)
        cols = slice(g * gv, (g + 1) * gv)
        sh = shifts[:, cols]
        start = vec[:, cols].astype(F32)
        resid = total - sh * start
        div = jnp.maximum(jnp.abs(den_col - sh), 1.0)
        update = (start - resid / div).astype(BF16)
        nextv[g] = update
        heldn[g, mine_rows, :] = update
        next_out[:, cols] = update
        got.append(gather_start(g))
    for g in range(2):
        gather_relay(g, got[g])
    for g in range(2):
        gather_end(g, got[g])
        spread(1, g, False)
    for g in range(2):
        relay(1, g)
    for g in range(2):
        first_sums(1, g)
    for g in range(2):
        prod_out[:, g * gv:(g + 1) * gv] = last_sums(1, g)
    for cp in pending:
        cp.wait_send()


def local(nx, nz, ny, kernel, intersection, momentum, owner_pick, live_count, pair_slot, denominators, shifts, vectors):
    pr, nv = vectors.shape
    nq, cb, fb = intersection.shape
    nc = 2 * ny
    gv = nv // 2
    hr = pr // 2
    rows = nx * nz * pr
    wide = nc * pr
    fr, fc = pair_slot.shape
    hop = ny // 2
    dma = pltpu.SemaphoreType.DMA
    hbm = pl.BlockSpec(memory_space=pltpu.HBM)
    vmem = pl.BlockSpec(memory_space=pltpu.VMEM)
    far = max(nx, nz)
    few = max(1, far // 2 - 1)
    prod, nextv = pl.pallas_call(
        functools.partial(body, nx, nz, ny, fb),
        out_shape=(jax.ShapeDtypeStruct((pr, nv), F32), jax.ShapeDtypeStruct((pr, nv), BF16)),
        in_specs=[hbm] * 9,
        out_specs=(vmem, vmem),
        scratch_shapes=[
            pltpu.SMEM(momentum.shape, jnp.int32),
            pltpu.SMEM(owner_pick.shape, jnp.int32),
            pltpu.SMEM(live_count.shape, jnp.int32),
            pltpu.SMEM((fc, fr), jnp.int32),
            pltpu.VMEM((1, pr), F32),
            pltpu.VMEM((1, nv), F32),
            pltpu.VMEM((pr, nv), BF16),
            pltpu.VMEM((nq, cb, fb), BF16),
            pltpu.VMEM((nc, 2, cb + hr, cb), BF16),
            pltpu.VMEM((nc + 1, cb, wide), BF16),
            pltpu.VMEM((cb, wide), BF16),
            pltpu.VMEM((rows, wide), BF16),
            pltpu.VMEM((wide, nv), BF16),
            pltpu.VMEM((2, wide, gv), BF16),
            pltpu.VMEM((2, pr, gv), BF16),
            pltpu.VMEM((nc, 8, 128), jnp.int32),
            pltpu.VMEM((8, 128), jnp.int32),
            pltpu.VMEM((2, 2, nx, nz * hr, gv), BF16),
            pltpu.VMEM((2, 2, nz, nx * hr, gv), BF16),
            pltpu.VMEM((2, 2, few, nz * hr, gv), BF16),
            pltpu.VMEM((2, 2, few, nx * hr, gv), BF16),
            pltpu.VMEM((2, 2, few, nz * hr, gv), BF16),
            pltpu.VMEM((2, 2, few, nx * hr, gv), BF16),
            pltpu.VMEM((2, 2, few + 1, nz * hr, gv), BF16),
            pltpu.VMEM((2, 2, few + 1, nx * hr, gv), BF16),
            pltpu.VMEM((2, 2, nz, hr, gv), BF16),
            pltpu.VMEM((2, 2, nx, hr, gv), BF16),
            pltpu.VMEM((2, 2, nz * hr, gv), BF16),
            pltpu.VMEM((2, 2, nx * hr, gv), BF16),
            pltpu.VMEM((2, nz * hr, gv), F32),
            pltpu.VMEM((2, nx * hr, gv), F32),
            dma((12,)),
            dma((2, ny)), dma((2, ny)),
            dma((2, ny)), dma((2, ny)),
            dma((2, hop, 2)), dma((2, hop, 2)),
            dma((2, hop + 1, 2)), dma((2, hop + 1, 2)),
            dma((2, hop)), dma((2, hop)),
            dma((2, hop + 1)), dma((2, hop + 1)),
            dma((2, 2, 2, few)), dma((2, 2, 2, few)),
            dma((2, 2, 2, few + 1)), dma((2, 2, 2, few + 1)),
            dma((2, 2, 2, far)), dma((2, 2, 2, far)),
        ],
        compiler_params=pltpu.CompilerParams(collective_id=0, has_side_effects=True, vmem_limit_bytes=67_043_328),
    )(
        momentum, owner_pick, live_count, pair_slot.T, intersection, kernel,
        denominators.reshape(1, pr), shifts.reshape(1, nv), vectors,
    )
    next_float = nextv.astype(F32)
    divisor = jnp.maximum(jnp.abs(denominators[:, None] - shifts[None, :]), 1.0)
    residual = prod - shifts[None, :] * next_float
    return next_float - residual / divisor, residual


def build(mesh, nx, nz, ny):
    whole = P(("row", "col"))
    return jax.shard_map(
        functools.partial(local, nx, nz, ny),
        mesh=mesh,
        in_specs=(
            P(("row", "col"), None, None), P(), P(), whole, whole, P(("row", "col"), None), whole, P(), P(("row", "col"), None),
        ),
        out_specs=(P(("row", "col"), None), P(("row", "col"), None)),
        check_vma=False,
    )


def solution(mesh):
    return build(mesh, 8, 8, mesh.shape["col"] // 2)
```

time: 110 us -> 94.6 us (0.86)
  Pallas kernels: 101 us -> 91 us
  local copies, waits for them, and re-layouts: 6.68 us -> 0 us
    pallas_call x1, Pallas kernels: 101 us -> 91 us  [local(): pl.pallas_call(functools.partial(body, nx, nz, ny, fb), out_shape=(jax.Sh...]
    unnamed x15 -> x0, local copies, waits for them, and re-layouts: 6.68 us -> none
where the time goes in v2:
time: 94.6 us; the launch traced here: 93.8 us
  Pallas kernels  91 us (96%)
  other arithmetic  1.51 us (2%)
  between operations  1.29 us (1%)
    pallas_call x1, Pallas kernels, local(): pl.pallas_call(functools.partial(body, nx, nz, ny, fb), out_shape=(jax.Sh...  91 us

profile of v2, /device:TPU:1, one launch (start us, length us, event | category | flops | bytes accessed | tf_op | source)
XLA Modules:
  0.0 93.8 jit_solution(1589420155941306965)
XLA Ops:
  1.3 91.0 %shard_map.104 = (f32[32,256]{1,0:T(8,128)}, bf16[32,256]{1,0:T(8,128)(2,1)}) custom-call(s32[256]{0:T(256)} %mom_hbm.1, s32[16]{0:T(128)} %picks_hbm.1, s32[1]{0:T(128)S(6)} %copy.11.live_hbm, s32[4,16]{1,0:T(4,128)} %bitcast.4, bf16[32,256,128]{2,1,0:T(8,128)(2,1)} %inter_hbm.1, bf16[2,256,256]{2,1,0:T(8,128)(2,1)} %kern_hbm.1, f32[1,32]{1,0:T(1,128)} %bitcast.5, ...), custom_call_target="tpu_custom_call" | custom-call | tf_op jit(solution)/shard_map/pallas_call | solution.py:401
  92.3 1.5 %convert_subtract_fusion = (f32[32,256]{1,0:T(8,128)}, f32[32,256]{1,0:T(8,128)}) fusion(bf16[32,256]{1,0:T(8,128)(2,1)} %get-tuple-element.4, f32[32]{0:T(128)} %param.15, f32[256]{0:T(256)} %param.16, f32[32,256]{1,0:T(8,128)} %get-tuple-element.5), kind=kLoop, calls=%fused_computation | loop fusion | flops 65536 | bytes 115840 | tf_op jit(solution)/shard_map/sub | solution.py:457

commit v3 on v2

--- a/solution.py
+++ b/solution.py
@@ -27,7 +27,7 @@
     mom_hbm, picks_hbm, live_hbm, slots_hbm, inter_hbm, kern_hbm, den_hbm, shifts_hbm, vec_hbm,
     prod_out, next_out,
     mom, picks, live, slots, den, shifts, vec,
-    inter, blk, half, basis, tile, held, heldn, nextv, pk, pk_own,
+    inter, turned, blk, half, basis, tile, held, heldn, nextv, pk, pk_own,
     part0, part1, near0, near1, pair0, pair1, rx0, rx1, ry0, ry1, sum0, sum1, acc0, acc1,
     loc, ag_s, ag_r, fw_s, fw_r, ring_s, ring_r, sib_s, sib_r, ringp_s, ringp_r, sibp_s, sibp_r,
     s0_s, s0_r, s1_s, s1_r, s2_s, s2_r,
@@ -143,18 +143,14 @@
             held[pl.ds(pl.multiple_of(src * pr + k * hr, hr), hr), :] = blk[src, k, cb:cb + hr]
 
     def halves(t):
+        if t == 0 or t == hop:
+            half_of((y if t == 0 else (y + hop) % ny) * 2 + core)
         for way in range(1 if t == 0 else 2):
             for k in range(2):
                 for cp in sib.get((way, t, k), []):
                     cp.wait_recv()
         if t == 0 or t == hop:
-            spot = y if t == 0 else (y + hop) % ny
-
-            def one(j, carry):
-                half_of(spot * 2 + j)
-                return carry
-
-            lax.fori_loop(0, 2, one, 0)
+            half_of((y if t == 0 else (y + hop) % ny) * 2 + 1 - core)
         else:
 
             def one(j, carry):
@@ -163,7 +159,18 @@
 
             lax.fori_loop(0, 4, one, 0)
 
+    def turn_rows():
+        def one(a, carry):
+            turned[a] = inter[mom[c * (nx * nblk) + a]].T
+            return carry
+
+        lax.fori_loop(0, nx * nblk, one, 0)
+
+    if hop == 0:
+        turn_rows()
     for t in range(1, hop + 1):
+        if t == hop:
+            halves(t - 1)
         for way, k in lanes:
             if t > length[way, k]:
                 continue
@@ -173,7 +180,10 @@
             if t < length[way, k]:
                 ring[way, t + 1, k] = pass_on(way, t, k, src, step_to[way], on_ring)
             sib[way, t, k] = pass_on(way, t, k, src, other, on_sib)
-        halves(t - 1)
+        if t < hop:
+            halves(t - 1)
+        if t == 1:
+            turn_rows()
     halves(hop)
     for many in list(ring.values()) + list(sib.values()):
         pending += many
@@ -205,21 +215,24 @@
                 slot = jnp.where(slot < live[0], slot, nc)
                 parts.append(half[slot, :, b * fb:(b + 1) * fb])
             picked = jnp.concatenate(parts, axis=1)
-            u = inter[mom[c * (nx * nblk) + a]]
-            fine = lax.dot_general(u, picked, (((0,), (0,)), ((), ())), preferred_element_type=F32)
+            fine = jnp.dot(turned[a], picked, preferred_element_type=F32)
             tile[pl.ds(pl.multiple_of(a * fb, fb), fb), :] = fine.astype(BF16)
 
     flight = {}
 
     def spread(p, g, build):
         def product(x2):
+            if p == 0 and not build:
+                return
             if build:
                 build_rows(x2)
-            v = held[:, g * gv:(g + 1) * gv] if p == 0 else heldn[g]
+            v = held[...] if build else heldn[g]
             got = jnp.dot(tile[tile_rows(x2), :], v, preferred_element_type=F32).astype(BF16)
-            for j in range(nz):
-                part0[p, g, x2, j * hr:(j + 1) * hr, :] = got[j * pr:j * pr + hr]
-                part1[p, g, j, pl.ds(pl.multiple_of(x2 * hr, hr), hr), :] = got[j * pr + hr:(j + 1) * pr]
+            for w in (0, 1) if build else (g,):
+                cols = slice(w * gv, (w + 1) * gv) if build else slice(0, gv)
+                for j in range(nz):
+                    part0[p, w, x2, j * hr:(j + 1) * hr, :] = got[j * pr:j * pr + hr, cols]
+                    part1[p, w, j, pl.ds(pl.multiple_of(x2 * hr, hr), hr), :] = got[j * pr + hr:(j + 1) * pr, cols]
 
         def far_copy(h, j, far, near):
             n, me = (nx, x) if h == 0 else (nz, z)
@@ -251,7 +264,8 @@
 
             lax.fori_loop(0, len(pairs), far_step, 0)
         start = len(pairs)
-        lax.fori_loop(0, nx - len(pairs), step, 0)
+        if p == 1 or build:
+            lax.fori_loop(0, nx - len(pairs), step, 0)
         direct = {}
         for h in range(2):
             n, me = (nx, x) if h == 0 else (nz, z)
@@ -412,6 +426,7 @@
             pltpu.VMEM((1, nv), F32),
             pltpu.VMEM((pr, nv), BF16),
             pltpu.VMEM((nq, cb, fb), BF16),
+            pltpu.VMEM((fr, fb, cb), BF16),
             pltpu.VMEM((nc, 2, cb + hr, cb), BF16),
             pltpu.VMEM((nc + 1, cb, wide), BF16),
             pltpu.VMEM((cb, wide), BF16),

time: 94.6 us -> 94.7 us (level)
  no operation moved by 1% of the time
where the time goes in v3:
time: 94.7 us; the launch traced here: 94.3 us
  Pallas kernels  91.5 us (97%)
  other arithmetic  1.51 us (2%)
  between operations  1.29 us (1%)
    pallas_call x1, Pallas kernels, local(): pl.pallas_call(functools.partial(body, nx, nz, ny, fb), out_shape=(jax.Sh...  91.5 us

profile of v3, /device:TPU:1, one launch (start us, length us, event | category | flops | bytes accessed | tf_op | source)
XLA Modules:
  0.0 94.3 jit_solution(9420730349897062949)
XLA Ops:
  1.3 91.5 %shard_map.104 = (f32[32,256]{1,0:T(8,128)}, bf16[32,256]{1,0:T(8,128)(2,1)}) custom-call(s32[256]{0:T(256)} %mom_hbm.1, s32[16]{0:T(128)} %picks_hbm.1, s32[1]{0:T(128)S(6)} %copy.11.live_hbm, s32[4,16]{1,0:T(4,128)} %bitcast.4, bf16[32,256,128]{2,1,0:T(8,128)(2,1)} %inter_hbm.1, bf16[2,256,256]{2,1,0:T(8,128)(2,1)} %kern_hbm.1, f32[1,32]{1,0:T(1,128)} %bitcast.5, ...), custom_call_target="tpu_custom_call" | custom-call | tf_op jit(solution)/shard_map/pallas_call | solution.py:415
  92.8 1.5 %convert_subtract_fusion = (f32[32,256]{1,0:T(8,128)}, f32[32,256]{1,0:T(8,128)}) fusion(bf16[32,256]{1,0:T(8,128)(2,1)} %get-tuple-element.4, f32[32]{0:T(128)} %param.15, f32[256]{0:T(256)} %param.16, f32[32,256]{1,0:T(8,128)} %get-tuple-element.5), kind=kLoop, calls=%fused_computation | loop fusion | flops 65536 | bytes 115840 | tf_op jit(solution)/shard_map/sub | solution.py:472
